TPU v7x, 128 devices: a whole 4x4x4 slice. The times are simulated.
128 devices in a mesh: tm: 4 (over x), op: 32 (over y, z, core).
Axes of the slice: x: 4, y: 4, z: 4, core: 2. Of those that a mesh axis runs over, the one named last changes fastest.
Arguments:
- sink_elem: bfloat16 [2, 4, 2048, 16384], P(None, 'tm', 'op'), may hold values from -6 to 6
- source_elem: bfloat16 [2, 2, 2048, 16384], P(None, None, None, 'op'), may hold values from -6 to 6
- peram: bfloat16 [2, 4, 2, 512, 512], P(None, 'tm', None, 'op'), may hold values from -4 to 4
- pair_list: int32 [16, 1], replicated, may hold values from 0 to 15
- spin_sets: int32 [16, 3], replicated, may hold values from 0 to 3
Outputs:
- correlator: float32 [2, 4, 2, 16, 1], P(None, 'tm')
All inputs are finite; a program needn't handle non-finite values.
Results may differ from a plain program's by a relative error of at most 0.0041.
Values may be sent and summed in bfloat16 or wider, within the bound.
A program may use at most 192 MiB of HBM per device.

v0:
```python
import jax
import jax.numpy as jnp
from jax import lax
from jax.sharding import PartitionSpec as P

NEV = 128
NSPIN = 4
NOP = 16
TSRC = 2
PAIRS = 1


def complex_matrix(block):
    upper = jnp.concatenate([block[0], block[1]], axis=1)
    lower = jnp.concatenate([-block[1], block[0]], axis=1)
    return jnp.stack([upper, lower])


def on_device(sink_elem, source_elem, peram, pair_list, spin_sets):
    tau_all = lax.all_gather(peram, "op", axis=3, tiled=True)
    position = lax.axis_index("op")
    rows = sink_elem.shape[2]
    local_times = sink_elem.shape[1]
    span = min(rows, NEV)
    cols = source_elem.shape[3]

    def spin_block(local, t0, left, right):
        return lax.dynamic_slice(tau_all[:, local, t0], (0, left * NEV, right * NEV), (2, NEV, NEV))

    def sink_side(local, t0, p):
        op_now = (position * rows + 0) // NEV
        mine = spin_sets[op_now]
        theirs = spin_sets[pair_list[op_now, p]]
        third = complex_matrix(spin_block(local, t0, mine[2], theirs[2]))
        second = complex_matrix(spin_block(local, t0, mine[1], theirs[1]))
        phi = sink_elem[:, local, 0:span].reshape(2, span * NEV, NEV)
        x_both = jnp.einsum("cxk,ckb->xb", phi, third, preferred_element_type=jnp.float32)
        x_both = x_both.astype(jnp.bfloat16).reshape(span, NEV, 2, NEV)
        y_both = jnp.einsum("ijck,cjb->ibk", x_both, second, preferred_element_type=jnp.float32)
        y_both = y_both.astype(jnp.bfloat16).reshape(span, 2, NEV * NEV)
        pieces = jnp.transpose(y_both, (1, 0, 2))
        return pieces

    partial_terms = {}
    combos = [
        (local, t0, p) for local in range(local_times) for t0 in range(TSRC) for p in range(PAIRS)
    ]
    stacked = jnp.stack([sink_side(local, t0, p) for local, t0, p in combos], axis=1)
    columns = lax.all_to_all(stacked, "op", split_axis=3, concat_axis=2, tiled=True)
    for index, combo in enumerate(combos):
        column_t0 = combo[1]
        other = pair_list[:, combo[2]]
        source = source_elem[:, column_t0].reshape(2, NOP, NEV, cols)
        chosen = jnp.take(source, other, axis=1)
        tiles = columns[:, index].reshape(2, NOP, NEV, cols)

        def inner(a, b):
            return jnp.einsum("oic,ojc->oij", a, b, preferred_element_type=jnp.float32)

        m_re = inner(tiles[0], chosen[0]) + inner(tiles[1], chosen[1])
        m_im = inner(tiles[1], chosen[0]) - inner(tiles[0], chosen[1])
        blocks = tau_all[:, combo[0], column_t0].reshape(2, NSPIN, NEV, NSPIN, NEV)
        blocks = jnp.transpose(blocks, (1, 3, 0, 2, 4))
        first = blocks[spin_sets[:, 0], spin_sets[other, 0]].astype(jnp.float32)
        c_re = jnp.sum(first[:, 0] * m_re - first[:, 1] * m_im, axis=(1, 2))
        c_im = jnp.sum(first[:, 0] * m_im + first[:, 1] * m_re, axis=(1, 2))
        partial_terms[combo] = jnp.stack([c_re, c_im])
    local = 0
    per_time = []
    for t0 in range(TSRC):
        per_time.append(jnp.stack([partial_terms[local, t0, 0]], axis=-1))
    per_local = [jnp.stack(per_time, axis=1)]
    partial_sum = jnp.stack(per_local, axis=1)
    totals = lax.psum(partial_sum, "op")
    return totals * (1.0 / float(NEV**3))


def solution(mesh):
    in_specs = (
        P(None, "tm", "op", None),
        P(None, None, None, "op"),
        P(None, "tm", None, "op", None),
        P(),
        P(),
    )
    out_specs = P(None, "tm", None, None, None)
    return jax.shard_map(
        on_device, mesh=mesh, in_specs=in_specs, out_specs=out_specs, check_vma=False
    )
```

profile of v0, /device:TPU:1, one launch (start us, length us, event | category | flops | bytes accessed | tf_op | source)
XLA Modules:
  0.0 462.1 jit_solution(5356037397111504323)
XLA Ops:
  15.2 7.4 %reshape_squeeze.19 = bf16[2,8192,128]{2,1,0:T(8,128)(2,1)} reshape(bf16[2,1,64,16384]{3,2,1,0:T(8,128)(2,1)} %param.7) | data formatting | bytes 8388608 | tf_op jit(solution)/shard_map/reshape;squeeze | solution.py:36
  22.6 34.7 %all-gather.2.cloned.1.call-done = bf16[2,1,2,512,512]{4,2,1,0,3:T(2,128)(2,1)} async-done(((bf16[2,1,2,16,512]{4,2,1,0,3:T(2,128)(2,1)}), bf16[2,1,2,512,512]{4,2,1,0,3:T(2,128)(2,1)}) %all-gather.2.cloned.1.call-update) | async-done | bytes 2097168 | tf_op jit(solution)/shard_map/all_gather | solution.py:20
  57.3 6.5 %fusion.57 = (bf16[2,1,1,512,512]{4,2,1,0,3:T(2,128)(2,1)}, bf16[2,1,1,512,512]{4,2,1,0,3:T(2,128)(2,1)S(1)}) fusion(bf16[2,1,2,512,512]{4,2,1,0,3:T(2,128)(2,1)} %all-gather.2.cloned.1.call-done), kind=kLoop, calls=%fused_computation.113 | loop fusion | bytes 4194304 | tf_op jit(solution)/shard_map/slice | solution.py:62
  63.8 4.6 copy.59
  68.4 4.2 copy.60
  78.9 7.4 %fusion.2 = bf16[64,256,128]{2,1,0:T(8,128)(2,1)} fusion(bf16[64,128,2,128]{1,0,3,2:T(8,128)(2,1)S(1)} %bitcast.218, bf16[1,128,256]{1,2,0:T(8,128)(2,1)S(1)} %get-tuple-element.35, bf16[1,128,256]{1,2,0:T(8,128)(2,1)S(1)} %get-tuple-element.34), kind=kOutput, calls=%fused_computation.12 | convolution fusion | flops 1076101120 | bytes 8519680 | tf_op jit(solution)/shard_map/ijck,cjb->ibk/dot_general | solution.py:39
  86.4 6.9 %reshape.75 = bf16[64,2,16384]{2,1,0:T(2,128)(2,1)} reshape(bf16[64,256,128]{2,1,0:T(8,128)(2,1)} %fusion.2) | data formatting | bytes 8388608 | tf_op jit(solution)/shard_map/reshape | solution.py:40
  93.2 6.6 %copy.83 = bf16[64,2,16384]{2,0,1:T(8,128)(2,1)} copy(bf16[64,2,16384]{2,1,0:T(2,128)(2,1)} %reshape.75) | data formatting | bytes 8388608 | tf_op jit(solution)/shard_map/reshape | solution.py:40
  102.4 7.4 %fusion.3 = bf16[64,256,128]{2,1,0:T(8,128)(2,1)} fusion(bf16[64,128,2,128]{1,0,3,2:T(8,128)(2,1)S(1)} %bitcast.219, bf16[1,128,256]{1,2,0:T(8,128)(2,1)S(1)} %get-tuple-element.39, bf16[1,128,256]{1,2,0:T(8,128)(2,1)S(1)} %get-tuple-element.38), kind=kOutput, calls=%fused_computation.13 | convolution fusion | flops 1076101120 | bytes 8519680 | tf_op jit(solution)/shard_map/ijck,cjb->ibk/dot_general | solution.py:39
  109.8 6.9 %reshape.77 = bf16[64,2,16384]{2,1,0:T(2,128)(2,1)} reshape(bf16[64,256,128]{2,1,0:T(8,128)(2,1)} %fusion.3) | data formatting | bytes 8388608 | tf_op jit(solution)/shard_map/reshape | solution.py:40
  116.7 6.6 %copy.82 = bf16[64,2,16384]{2,0,1:T(8,128)(2,1)} copy(bf16[64,2,16384]{2,1,0:T(2,128)(2,1)} %reshape.77) | data formatting | bytes 8388608 | tf_op jit(solution)/shard_map/reshape | solution.py:40
  123.3 6.2 %pad_maximum_fusion = bf16[2,2,64,16384]{3,2,1,0:T(8,128)(2,1)} fusion(bf16[2,1,64,16384]{3,2,1,0:T(8,128)(2,1)} %bitcast.222, bf16[2,1,64,16384]{3,2,1,0:T(8,128)(2,1)S(1)} %bitcast.220), kind=kLoop, calls=%fused_computation.9 | loop fusion | flops 4194304 | bytes 16777216 | tf_op jit(solution)/shard_map/stack | solution.py:48
  129.5 34.5 %copy.49 = bf16[2,2,64,16384]{2,1,0,3:T(2,128)(2,1)} copy(bf16[2,2,64,16384]{3,2,1,0:T(8,128)(2,1)} %pad_maximum_fusion) | data formatting | bytes 16777216 | tf_op jit(solution)/shard_map/stack | solution.py:48
  164.0 26.7 %reshape.124 = bf16[32,2,65536]{2,1,0:T(2,128)(2,1)} reshape(bf16[16384,2,2,64]{3,2,1,0:T(2,128)(2,1)} %bitcast.211) | data formatting | bytes 16777216
  190.7 5.4 %all-to-all-start = ((bf16[32,2,65536]{2,1,0:T(2,128)(2,1)}), bf16[32,2,65536]{2,1,0:T(2,128)(2,1)}, u32[]{:S(2)}, u32[]{:S(2)}) async-start(bf16[32,2,65536]{2,1,0:T(2,128)(2,1)} %reshape.124), calls=%async_computation | async-start | bytes 16777216 | tf_op jit(solution)/shard_map/all_to_all | solution.py:49
  196.2 5.8 %fusion.56 = (bf16[2,1,2048,512]{3,2,1,0:T(8,128)(2,1)}, bf16[2,1,2048,512]{3,2,1,0:T(8,128)(2,1)}) fusion(bf16[2,2,2048,512]{3,2,1,0:T(8,128)(2,1)} %param.8), kind=kLoop, calls=%fused_computation.112 | loop fusion | bytes 16777216 | tf_op jit(solution)/shard_map/slice | solution.py:53
  202.0 5.0 %gather_fusion.3 = bf16[16,2,128,512]{3,2,1,0:T(8,128)(2,1)} fusion(bf16[2,16,128,512]{3,2,1,0:T(8,128)(2,1)} %bitcast.223, s32[1024]{0:T(1024)S(1)} %pad_clamp_fusion), kind=kCustom, calls=%fused_computation.clone | custom fusion | bytes 8388672 | tf_op jit(solution)/shard_map/jit(_take)/gather | solution.py:54
  207.0 5.0 %gather_fusion.4 = bf16[16,2,128,512]{3,2,1,0:T(8,128)(2,1)} fusion(bf16[2,16,128,512]{3,2,1,0:T(8,128)(2,1)} %bitcast.221, s32[1024]{0:T(1024)S(1)} %pad_clamp_fusion), kind=kCustom, calls=%fused_computation.1.clone | custom fusion | bytes 8388672 | tf_op jit(solution)/shard_map/jit(_take)/gather | solution.py:54
  212.7 6.0 %fusion.5 = (bf16[2,16,128,512]{3,2,1,0:T(8,128)(2,1)}, bf16[2,16,128,512]{3,2,1,0:T(8,128)(2,1)}) fusion(bf16[16,2,128,512]{3,2,1,0:T(8,128)(2,1)} %gather_fusion.3, pred[16]{0:T(512)(128)(4,1)S(1)} %compare_and_fusion, bf16[16,2,128,512]{3,2,1,0:T(8,128)(2,1)} %gather_fusion.4), kind=kLoop, calls=%fused_computation.17 | loop fusion | flops 4194304 | bytes 16777232 | tf_op jit(solution)/shard_map/jit(_take)/select_n | solution.py:54
  229.2 75.5 %all-to-all-done = bf16[32,2,65536]{2,1,0:T(2,128)(2,1)} async-done(((bf16[32,2,65536]{2,1,0:T(2,128)(2,1)}), bf16[32,2,65536]{2,1,0:T(2,128)(2,1)}, u32[]{:S(2)}, u32[]{:S(2)}) %all-to-all-start) | async-done | bytes 8388640 | tf_op jit(solution)/shard_map/all_to_all | solution.py:49
  304.7 26.0 %reshape.125 = bf16[16384,2,2,64]{3,2,1,0:T(2,128)(2,1)} reshape(bf16[32,2,65536]{2,1,0:T(2,128)(2,1)} %all-to-all-done) | data formatting | bytes 16777216
  330.7 36.1 %copy.50 = bf16[2,2,32,64,512]{4,3,2,1,0:T(8,128)(2,1)} copy(bf16[2,2,32,64,512]{3,1,0,4,2:T(2,128)(2,1)} %bitcast.212) | data formatting | bytes 16777216 | tf_op jit(solution)/shard_map/all_to_all | solution.py:49
  366.8 4.0 fusion.55
  380.5 74.2 %psum.7 = f32[2,1,2,16,1]{3,2,0,4,1:T(2,128)S(1)} all-reduce(f32[2,1,2,16,1]{3,2,0,4,1:T(2,128)S(1)} %bitcast.230), channel_id=1, replica_groups=mesh['tm'=4,'op'=32] {'op'}, use_global_device_ids=true, to_apply=%region_4.6 | all-reduce | flops 64 | bytes 512 | tf_op jit(solution)/shard_map/psum | solution.py:74
  (63 shorter events, 34.6 us)
Async XLA Ops:
  6.5 50.8 %all-gather.2.cloned.1.call-start = ((), (), s32[]{:S(2)}) async-start(), calls=%async_computation.1 | async-start | bytes 2162688 | tf_op jit(solution)/shard_map/all_gather | solution.py:20
  93.2 6.6 %copy-start.1 = (bf16[2,8192,128]{2,1,0:T(8,128)(2,1)S(1)}, bf16[2,8192,128]{2,1,0:T(8,128)(2,1)}, u32[]{:S(2)}) copy-start(bf16[2,8192,128]{2,1,0:T(8,128)(2,1)} %reshape_squeeze.19) | copy-start | bytes 12582916
  116.7 6.6 %copy-start.4 = (bf16[64,2,16384]{2,0,1:T(8,128)(2,1)S(1)}, bf16[64,2,16384]{2,0,1:T(8,128)(2,1)}, u32[]{:S(2)}) copy-start(bf16[64,2,16384]{2,0,1:T(8,128)(2,1)} %copy.83) | copy-start | bytes 12582916
  190.7 5.4 %copy-start.8 = (s32[16,1]{0,1:T(1,128)S(1)}, s32[16,1]{0,1:T(1,128)}, u32[]{:S(2)}) copy-start(s32[16,1]{0,1:T(1,128)} %param.10) | copy-start | bytes 196
  190.7 114.0 %all-to-all-start = ((bf16[32,2,65536]{2,1,0:T(2,128)(2,1)}), bf16[32,2,65536]{2,1,0:T(2,128)(2,1)}, u32[]{:S(2)}, u32[]{:S(2)}) async-start(bf16[32,2,65536]{2,1,0:T(2,128)(2,1)} %reshape.124), calls=%async_computation | async-start | bytes 16777216 | tf_op jit(solution)/shard_map/all_to_all | solution.py:49
  207.0 5.0 %copy-start = (s32[16,3]{0,1:T(4,128)S(1)}, s32[16,3]{0,1:T(4,128)}, u32[]{:S(2)}) copy-start(s32[16,3]{0,1:T(4,128)} %param.11) | copy-start | bytes 580
  212.7 6.3 %copy-start.5 = (bf16[2,1,1,512,512]{3,4,2,1,0:T(8,128)(2,1)S(1)}, bf16[2,1,1,512,512]{3,4,2,1,0:T(8,128)(2,1)}, u32[]{:S(2)}) copy-start(bf16[2,1,1,512,512]{3,4,2,1,0:T(8,128)(2,1)} %copy.60) | copy-start | bytes 3145732
  366.8 4.7 %copy-start.3 = (bf16[2,16,128,512]{3,2,1,0:T(8,128)(2,1)S(1)}, bf16[2,16,128,512]{3,2,1,0:T(8,128)(2,1)}, u32[]{:S(2)}) copy-start(bf16[2,16,128,512]{3,2,1,0:T(8,128)(2,1)} %get-tuple-element.48) | copy-start | bytes 12582916
  372.8 2.2 copy-start.2
  376.5 1.6 copy-start.7
  378.0 1.6 copy-start.6
Sparse Core Ops, SparseCore 0:
  9.6 47.6 all-gather.1
where the time goes:
time: 467 us; the launch traced here: 462 us
  local copies, waits for them, and re-layouts  212 us (45%)
  waiting for transfers between devices  110 us (24%)
  blocking collectives  74.2 us (16%)
  matrix products  25.6 us (5%)
  between operations  18.1 us (4%)
  other arithmetic  16.8 us (4%)
  starting transfers between devices  5.43 us (1%)
    all_to_all x1, waiting for transfers between devices, on_device(): lax.all_to_all(stacked, 'op', split_axis=3, concat_axis=2, tiled=True)  75.5 us
    psum x1, blocking collectives, on_device(): totals = lax.psum(partial_sum, 'op')  74.2 us
    unnamed x25, local copies, waits for them, and re-layouts  69.1 us
    all_to_all x1, local copies, waits for them, and re-layouts, on_device(): lax.all_to_all(stacked, 'op', split_axis=3, concat_axis=2, tiled=True)  36.1 us
    all_gather x1, waiting for transfers between devices, on_device(): tau_all = lax.all_gather(peram, 'op', axis=3, tiled=True)  34.7 us
    another operation x1, local copies, waits for them, and re-layouts, on_device(): jnp.stack([sink_side(local, t0, p) for local, t0, p in combos], axis=1)  34.5 us
    reshape x4, local copies, waits for them, and re-layouts, sink_side(): y_both = y_both.astype(jnp.bfloat16).reshape(span, 2, NEV * NEV)  27 us
    dot_general x2, matrix products, sink_side(): jnp.einsum('ijck,cjb->ibk', x_both, second, preferred_element_type=jnp.fl...  14.9 us
  transfers between devices with their start and end apart: 2, of which 2 were waited for; matrix products, arithmetic and copies ran while one was open for 9% of the time, Pallas kernels for 0%

commit v1 on v0

--- a/solution.py
+++ b/solution.py
@@ -71,7 +71,9 @@
         per_time.append(jnp.stack([partial_terms[local, t0, 0]], axis=-1))
     per_local = [jnp.stack(per_time, axis=1)]
     partial_sum = jnp.stack(per_local, axis=1)
-    totals = lax.psum(partial_sum, "op")
+    totals = partial_sum
+    for hop in (1, 2, 4, 8, 16):
+        totals = totals + lax.ppermute(totals, "op", [(dev, dev ^ hop) for dev in range(32)])
     return totals * (1.0 / float(NEV**3))
 
 

time: 467 us -> 426 us (0.912)
  blocking collectives: 74.2 us -> 0 us
  starting transfers between devices: 5.43 us -> 27 us
  waiting for transfers between devices: 110 us -> 118 us
    psum x1 -> x0, blocking collectives: 74.2 us -> none  [on_device(): totals = lax.psum(partial_sum, 'op')]
    ppermute x0 -> x5, starting transfers between devices: none -> 21.6 us  [on_device(): lax.ppermute(totals, 'op', [(dev, dev ^ hop) for dev in range(32)])]
    ppermute x0 -> x5, waiting for transfers between devices: none -> 9.59 us  [on_device(): lax.ppermute(totals, 'op', [(dev, dev ^ hop) for dev in range(32)])]
  transfers between devices with their start and end apart: 2 -> 7, of which waited for: 2 -> 7; matrix products, arithmetic and copies ran while one was open for 9% -> 10% of each run, Pallas kernels for 0% -> 0%
where the time goes in v1:
time: 426 us; the launch traced here: 418 us
  local copies, waits for them, and re-layouts  212 us (50%)
  waiting for transfers between devices  118 us (28%)
  starting transfers between devices  27 us (6%)
  matrix products  25.6 us (6%)
  between operations  18.2 us (4%)
  other arithmetic  17 us (4%)
    all_to_all x1, waiting for transfers between devices, on_device(): lax.all_to_all(stacked, 'op', split_axis=3, concat_axis=2, tiled=True)  74 us
    unnamed x25, local copies, waits for them, and re-layouts  69.1 us
    all_to_all x1, local copies, waits for them, and re-layouts, on_device(): lax.all_to_all(stacked, 'op', split_axis=3, concat_axis=2, tiled=True)  36 us
    all_gather x1, waiting for transfers between devices, on_device(): tau_all = lax.all_gather(peram, 'op', axis=3, tiled=True)  34.6 us
    another operation x1, local copies, waits for them, and re-layouts, on_device(): jnp.stack([sink_side(local, t0, p) for local, t0, p in combos], axis=1)  34.5 us
    reshape x4, local copies, waits for them, and re-layouts, sink_side(): y_both = y_both.astype(jnp.bfloat16).reshape(span, 2, NEV * NEV)  27 us
    ppermute x5, starting transfers between devices, on_device(): lax.ppermute(totals, 'op', [(dev, dev ^ hop) for dev in range(32)])  21.6 us
    dot_general x2, matrix products, sink_side(): jnp.einsum('ijck,cjb->ibk', x_both, second, preferred_element_type=jnp.fl...  14.9 us
  transfers between devices with their start and end apart: 7, of which 7 were waited for; matrix products, arithmetic and copies ran while one was open for 10% of the time, Pallas kernels for 0%

profile of v1, /device:TPU:1, one launch (start us, length us, event | category | flops | bytes accessed | tf_op | source)
XLA Modules:
  0.0 417.9 jit_solution(4791345972451215527)
XLA Ops:
  15.3 7.4 %reshape_squeeze.19 = bf16[2,8192,128]{2,1,0:T(8,128)(2,1)} reshape(bf16[2,1,64,16384]{3,2,1,0:T(8,128)(2,1)} %param.7) | data formatting | bytes 8388608 | tf_op jit(solution)/shard_map/reshape;squeeze | solution.py:36
  22.7 34.6 %all-gather.2.cloned.1.call-done = bf16[2,1,2,512,512]{4,2,1,0,3:T(2,128)(2,1)} async-done(((bf16[2,1,2,16,512]{4,2,1,0,3:T(2,128)(2,1)}), bf16[2,1,2,512,512]{4,2,1,0,3:T(2,128)(2,1)}) %all-gather.2.cloned.1.call-update) | async-done | bytes 2097168 | tf_op jit(solution)/shard_map/all_gather | solution.py:20
  57.3 6.6 %fusion.58 = (bf16[2,1,1,512,512]{4,2,1,0,3:T(2,128)(2,1)}, bf16[2,1,1,512,512]{4,2,1,0,3:T(2,128)(2,1)S(1)}) fusion(bf16[2,1,2,512,512]{4,2,1,0,3:T(2,128)(2,1)} %all-gather.2.cloned.1.call-done), kind=kLoop, calls=%fused_computation.114 | loop fusion | bytes 4194304 | tf_op jit(solution)/shard_map/slice | solution.py:62
  63.9 4.6 %copy.59 = bf16[2,1,1,512,512]{3,4,2,1,0:T(8,128)(2,1)S(1)} copy(bf16[2,1,1,512,512]{4,2,1,0,3:T(2,128)(2,1)} %get-tuple-element.24) | data formatting | bytes 2097152
  68.5 4.2 %copy.60 = bf16[2,1,1,512,512]{3,4,2,1,0:T(8,128)(2,1)} copy(bf16[2,1,1,512,512]{4,2,1,0,3:T(2,128)(2,1)S(1)} %get-tuple-element.25) | data formatting | bytes 2097152
  79.0 7.5 %fusion.2 = bf16[64,256,128]{2,1,0:T(8,128)(2,1)} fusion(bf16[64,128,2,128]{1,0,3,2:T(8,128)(2,1)S(1)} %bitcast.220, bf16[1,128,256]{1,2,0:T(8,128)(2,1)S(1)} %get-tuple-element.35, bf16[1,128,256]{1,2,0:T(8,128)(2,1)S(1)} %get-tuple-element.34), kind=kOutput, calls=%fused_computation.12 | convolution fusion | flops 1076101120 | bytes 8519680 | tf_op jit(solution)/shard_map/ijck,cjb->ibk/dot_general | solution.py:39
  86.5 6.9 %reshape.75 = bf16[64,2,16384]{2,1,0:T(2,128)(2,1)} reshape(bf16[64,256,128]{2,1,0:T(8,128)(2,1)} %fusion.2) | data formatting | bytes 8388608 | tf_op jit(solution)/shard_map/reshape | solution.py:40
  93.4 6.7 %copy.85 = bf16[64,2,16384]{2,0,1:T(8,128)(2,1)} copy(bf16[64,2,16384]{2,1,0:T(2,128)(2,1)} %reshape.75) | data formatting | bytes 8388608 | tf_op jit(solution)/shard_map/reshape | solution.py:40
  102.6 7.4 %fusion.3 = bf16[64,256,128]{2,1,0:T(8,128)(2,1)} fusion(bf16[64,128,2,128]{1,0,3,2:T(8,128)(2,1)S(1)} %bitcast.221, bf16[1,128,256]{1,2,0:T(8,128)(2,1)S(1)} %get-tuple-element.39, bf16[1,128,256]{1,2,0:T(8,128)(2,1)S(1)} %get-tuple-element.38), kind=kOutput, calls=%fused_computation.13 | convolution fusion | flops 1076101120 | bytes 8519680 | tf_op jit(solution)/shard_map/ijck,cjb->ibk/dot_general | solution.py:39
  110.0 6.9 %reshape.77 = bf16[64,2,16384]{2,1,0:T(2,128)(2,1)} reshape(bf16[64,256,128]{2,1,0:T(8,128)(2,1)} %fusion.3) | data formatting | bytes 8388608 | tf_op jit(solution)/shard_map/reshape | solution.py:40
  116.9 6.6 %copy.84 = bf16[64,2,16384]{2,0,1:T(8,128)(2,1)} copy(bf16[64,2,16384]{2,1,0:T(2,128)(2,1)} %reshape.77) | data formatting | bytes 8388608 | tf_op jit(solution)/shard_map/reshape | solution.py:40
  123.5 6.2 %pad_maximum_fusion = bf16[2,2,64,16384]{3,2,1,0:T(8,128)(2,1)} fusion(bf16[2,1,64,16384]{3,2,1,0:T(8,128)(2,1)} %bitcast.224, bf16[2,1,64,16384]{3,2,1,0:T(8,128)(2,1)S(1)} %bitcast.222), kind=kLoop, calls=%fused_computation.9 | loop fusion | flops 4194304 | bytes 16777216 | tf_op jit(solution)/shard_map/stack | solution.py:48
  129.7 34.5 %copy.49 = bf16[2,2,64,16384]{2,1,0,3:T(2,128)(2,1)} copy(bf16[2,2,64,16384]{3,2,1,0:T(8,128)(2,1)} %pad_maximum_fusion) | data formatting | bytes 16777216 | tf_op jit(solution)/shard_map/stack | solution.py:48
  164.2 26.7 %reshape.124 = bf16[32,2,65536]{2,1,0:T(2,128)(2,1)} reshape(bf16[16384,2,2,64]{3,2,1,0:T(2,128)(2,1)} %bitcast.213) | data formatting | bytes 16777216
  190.9 5.4 %all-to-all-start = ((bf16[32,2,65536]{2,1,0:T(2,128)(2,1)}), bf16[32,2,65536]{2,1,0:T(2,128)(2,1)}, u32[]{:S(2)}, u32[]{:S(2)}) async-start(bf16[32,2,65536]{2,1,0:T(2,128)(2,1)} %reshape.124), calls=%async_computation | async-start | bytes 16777216 | tf_op jit(solution)/shard_map/all_to_all | solution.py:49
  196.4 5.8 %fusion.57 = (bf16[2,1,2048,512]{3,2,1,0:T(8,128)(2,1)}, bf16[2,1,2048,512]{3,2,1,0:T(8,128)(2,1)}) fusion(bf16[2,2,2048,512]{3,2,1,0:T(8,128)(2,1)} %param.8), kind=kLoop, calls=%fused_computation.113 | loop fusion | bytes 16777216 | tf_op jit(solution)/shard_map/slice | solution.py:53
  202.2 4.9 %gather_fusion.3 = bf16[16,2,128,512]{3,2,1,0:T(8,128)(2,1)} fusion(bf16[2,16,128,512]{3,2,1,0:T(8,128)(2,1)} %bitcast.225, s32[1024]{0:T(1024)S(1)} %pad_clamp_fusion), kind=kCustom, calls=%fused_computation.clone | custom fusion | bytes 8388672 | tf_op jit(solution)/shard_map/jit(_take)/gather | solution.py:54
  207.1 5.0 %gather_fusion.4 = bf16[16,2,128,512]{3,2,1,0:T(8,128)(2,1)} fusion(bf16[2,16,128,512]{3,2,1,0:T(8,128)(2,1)} %bitcast.223, s32[1024]{0:T(1024)S(1)} %pad_clamp_fusion), kind=kCustom, calls=%fused_computation.1.clone | custom fusion | bytes 8388672 | tf_op jit(solution)/shard_map/jit(_take)/gather | solution.py:54
  212.9 6.1 %fusion.5 = (bf16[2,16,128,512]{3,2,1,0:T(8,128)(2,1)}, bf16[2,16,128,512]{3,2,1,0:T(8,128)(2,1)}) fusion(bf16[16,2,128,512]{3,2,1,0:T(8,128)(2,1)} %gather_fusion.3, pred[16]{0:T(512)(128)(4,1)S(1)} %compare_and_fusion, bf16[16,2,128,512]{3,2,1,0:T(8,128)(2,1)} %gather_fusion.4), kind=kLoop, calls=%fused_computation.17 | loop fusion | flops 4194304 | bytes 16777232 | tf_op jit(solution)/shard_map/jit(_take)/select_n | solution.py:54
  229.4 74.0 %all-to-all-done = bf16[32,2,65536]{2,1,0:T(2,128)(2,1)} async-done(((bf16[32,2,65536]{2,1,0:T(2,128)(2,1)}), bf16[32,2,65536]{2,1,0:T(2,128)(2,1)}, u32[]{:S(2)}, u32[]{:S(2)}) %all-to-all-start) | async-done | bytes 8388640 | tf_op jit(solution)/shard_map/all_to_all | solution.py:49
  303.5 26.0 %reshape.125 = bf16[16384,2,2,64]{3,2,1,0:T(2,128)(2,1)} reshape(bf16[32,2,65536]{2,1,0:T(2,128)(2,1)} %all-to-all-done) | data formatting | bytes 16777216
  329.5 36.0 %copy.50 = bf16[2,2,32,64,512]{4,3,2,1,0:T(8,128)(2,1)} copy(bf16[2,2,32,64,512]{3,1,0,4,2:T(2,128)(2,1)} %bitcast.214) | data formatting | bytes 16777216 | tf_op jit(solution)/shard_map/all_to_all | solution.py:49
  379.2 7.1 %collective-permute-start = (f32[2,1,2,16,1]{3,2,0,4,1:T(2,128)S(1)}, f32[2,1,2,16,1]{3,2,0,4,1:T(2,128)S(1)}, u32[]{:S(2)}, u32[]{:S(2)}) collective-permute-start(f32[2,1,2,16,1]{3,2,0,4,1:T(2,128)S(1)} %bitcast.232), channel_id=1, source_target_pairs={{0,1},{1,0},{2,3},{3,2},{4,5},{5,4},{6,7},{7,6},{8,9},{9,8},{10,11... | collective-permute-start | bytes 776 | tf_op jit(solution)/shard_map/ppermute | solution.py:76
  387.1 12.0 %collective-permute-start.1 = (f32[2,1,2,16,1]{3,2,0,4,1:T(2,128)S(1)}, f32[2,1,2,16,1]{3,2,0,4,1:T(2,128)S(1)}, u32[]{:S(2)}, u32[]{:S(2)}) collective-permute-start(f32[2,1,2,16,1]{3,2,0,4,1:T(2,128)S(1)} %fusion.51), channel_id=1, source_target_pairs={{0,2},{1,3},{2,0},{3,1},{4,6},{5,7},{6,4},{7,5},{8,10},{9,11},{10,... | collective-permute-start | bytes 776 | tf_op jit(solution)/shard_map/ppermute | solution.py:76
  (76 shorter events, 50.6 us)
Async XLA Ops:
  6.5 50.8 %all-gather.2.cloned.1.call-start = ((), (), s32[]{:S(2)}) async-start(), calls=%async_computation.1 | async-start | bytes 2162688 | tf_op jit(solution)/shard_map/all_gather | solution.py:20
  93.4 6.7 %copy-start.1 = (bf16[2,8192,128]{2,1,0:T(8,128)(2,1)S(1)}, bf16[2,8192,128]{2,1,0:T(8,128)(2,1)}, u32[]{:S(2)}) copy-start(bf16[2,8192,128]{2,1,0:T(8,128)(2,1)} %reshape_squeeze.19) | copy-start | bytes 12582916
  116.9 6.6 %copy-start.4 = (bf16[64,2,16384]{2,0,1:T(8,128)(2,1)S(1)}, bf16[64,2,16384]{2,0,1:T(8,128)(2,1)}, u32[]{:S(2)}) copy-start(bf16[64,2,16384]{2,0,1:T(8,128)(2,1)} %copy.85) | copy-start | bytes 12582916
  190.9 5.4 %copy-start.8 = (s32[16,1]{0,1:T(1,128)S(1)}, s32[16,1]{0,1:T(1,128)}, u32[]{:S(2)}) copy-start(s32[16,1]{0,1:T(1,128)} %param.10) | copy-start | bytes 196
  190.9 112.6 %all-to-all-start = ((bf16[32,2,65536]{2,1,0:T(2,128)(2,1)}), bf16[32,2,65536]{2,1,0:T(2,128)(2,1)}, u32[]{:S(2)}, u32[]{:S(2)}) async-start(bf16[32,2,65536]{2,1,0:T(2,128)(2,1)} %reshape.124), calls=%async_computation | async-start | bytes 16777216 | tf_op jit(solution)/shard_map/all_to_all | solution.py:49
  207.1 5.0 %copy-start = (s32[16,3]{0,1:T(4,128)S(1)}, s32[16,3]{0,1:T(4,128)}, u32[]{:S(2)}) copy-start(s32[16,3]{0,1:T(4,128)} %param.11) | copy-start | bytes 580
  212.8 6.4 %copy-start.5 = (bf16[2,1,1,512,512]{3,4,2,1,0:T(8,128)(2,1)S(1)}, bf16[2,1,1,512,512]{3,4,2,1,0:T(8,128)(2,1)}, u32[]{:S(2)}) copy-start(bf16[2,1,1,512,512]{3,4,2,1,0:T(8,128)(2,1)} %copy.60) | copy-start | bytes 3145732
  365.5 4.7 %copy-start.3 = (bf16[2,16,128,512]{3,2,1,0:T(8,128)(2,1)S(1)}, bf16[2,16,128,512]{3,2,1,0:T(8,128)(2,1)}, u32[]{:S(2)}) copy-start(bf16[2,16,128,512]{3,2,1,0:T(8,128)(2,1)} %get-tuple-element.48) | copy-start | bytes 12582916
  371.6 2.2 copy-start.2
  375.2 1.6 copy-start.7
  376.8 1.6 copy-start.6
  379.2 7.9 %collective-permute-start = (f32[2,1,2,16,1]{3,2,0,4,1:T(2,128)S(1)}, f32[2,1,2,16,1]{3,2,0,4,1:T(2,128)S(1)}, u32[]{:S(2)}, u32[]{:S(2)}) collective-permute-start(f32[2,1,2,16,1]{3,2,0,4,1:T(2,128)S(1)} %bitcast.232), channel_id=1, source_target_pairs={{0,1},{1,0},{2,3},{3,2},{4,5},{5,4},{6,7},{7,6},{8,9},{9,8},{10,11... | collective-permute-start | bytes 776 | tf_op jit(solution)/shard_map/ppermute | solution.py:76
  387.1 13.0 %collective-permute-start.1 = (f32[2,1,2,16,1]{3,2,0,4,1:T(2,128)S(1)}, f32[2,1,2,16,1]{3,2,0,4,1:T(2,128)S(1)}, u32[]{:S(2)}, u32[]{:S(2)}) collective-permute-start(f32[2,1,2,16,1]{3,2,0,4,1:T(2,128)S(1)} %fusion.51), channel_id=1, source_target_pairs={{0,2},{1,3},{2,0},{3,1},{4,6},{5,7},{6,4},{7,5},{8,10},{9,11},{10,... | collective-permute-start | bytes 776 | tf_op jit(solution)/shard_map/ppermute | solution.py:76
  400.1 3.9 collective-permute-start.2
  404.0 2.4 collective-permute-start.3
  406.5 3.9 collective-permute-start.4
Sparse Core Ops, SparseCore 0:
  9.6 47.6 all-gather.1
